TPU v7x, 128 devices: a whole 4x4x4 slice. The times are simulated.
128 devices in a mesh: dp: 64 (over y, z_hi, x, core), mp: 2 (over z_lo).
Axes of the slice: x: 4, y: 4, z: 4 (z_hi: 2, z_lo: 2; z = z_hi * 2 + z_lo), core: 2. Of those that a mesh axis runs over, the one named last changes fastest.
Arguments:
- belief: bfloat16 [16384, 2652], P('dp'), may hold values from -6 to 6
- target_value: bfloat16 [16384, 1326], P('dp'), may hold values from -6 to 6
- counts: int32 [128], P('dp'), may hold values from 1 to 128, as said below
- w_first: bfloat16 [2652, 1536], P(None, 'mp'), may hold values from -0.125 to 0.125
- w_middle: bfloat16 [1536, 1536], P('mp'), may hold values from -0.15625 to 0.15625
- w_last: bfloat16 [1536, 1326], P(None, 'mp'), may hold values from -0.15625 to 0.15625
Outputs:
- grad_first: float32 [2652, 1536], P(None, ('mp', 'dp'))
- grad_middle: float32 [1536, 1536], P('mp', 'dp')
- grad_last: float32 [1536, 1326], P('dp', 'mp')
Inputs may be any that keep to these rules, and one draw needn't show every extreme that they name: `counts`: rows past a subgame's count in its block are padding with arbitrary values.
All inputs are finite; a program needn't handle non-finite values.
Results may differ from a plain program's by a relative error of at most 0.0089.
Values may be sent and summed in bfloat16 or wider, within the bound.
No kernel may reach another device: no remote copies, remote signals or barrier semaphores. Data moves between devices by JAX's collectives and lax.ppermute only.
A program may use at most 192 MiB of HBM per device.

v0:
```python
import jax
import jax.numpy as jnp
from jax import lax
from jax.sharding import Mesh
from jax.sharding import PartitionSpec as P

BLOCK = 128
PARAMS = 8469504
DP = ("dp_0", "dp_1", "dp_2", "dp_3")
DP_MP = ("dp_0", "dp_1", "dp_2", "dp_3", "mp")
MP_DP = ("mp", "dp_0", "dp_1", "dp_2", "dp_3")


def copy_for_each(shard, axis):
    size = lax.axis_size(axis)
    return lax.all_to_all(
        jnp.broadcast_to(shard[None], (size, *shard.shape)), axis, 0, 0, tiled=True
    )


def taken_together(shard, axis):
    return copy_for_each(shard, axis).astype(jnp.float32).sum(axis=0)


def cut_along(shard, dim, size):
    lengths = shard.shape
    blocks = shard.reshape(*lengths[:dim], size, lengths[dim] // size, *lengths[dim + 1 :])
    return jnp.moveaxis(blocks, dim, 0)


def sum_at_owner(shard, axis, dim):
    size = lax.axis_size(axis)
    blocks = lax.all_to_all(cut_along(shard, dim, size), axis, 0, 0, tiled=True)
    return jnp.sum(blocks.astype(jnp.float32), axis=0)


def one_axis_at_a_time(shard, axes):
    for axis in axes:
        shard = lax.psum(shard, axis)
    return shard


def silu_slope(pre_act):
    sigmoid_of = jax.nn.sigmoid(pre_act)
    return sigmoid_of * (1.0 + pre_act * (1.0 - sigmoid_of))


def rows_grads(belief, target_value, live_mask, w_first, w_middle, w_last):
    pre_first = jnp.dot(belief, w_first, preferred_element_type=jnp.float32)
    act_first = jax.nn.silu(pre_first).astype(jnp.bfloat16)
    partial_middle = jnp.dot(act_first, w_middle, preferred_element_type=jnp.float32)
    pre_middle = taken_together(partial_middle.astype(jnp.bfloat16), "mp").astype(jnp.float32)
    act_middle = jax.nn.silu(pre_middle).astype(jnp.bfloat16)
    predicted = jnp.dot(act_middle, w_last, preferred_element_type=jnp.float32)
    mismatch = predicted - target_value.astype(jnp.float32)
    slope_out = (jnp.clip(mismatch, -1.0, 1.0) * live_mask[:, None]).astype(jnp.bfloat16)
    raw_last = jnp.dot(act_middle.T, slope_out, preferred_element_type=jnp.float32)
    partial_back = jnp.dot(slope_out, w_last.T, preferred_element_type=jnp.float32)
    back_middle = taken_together(partial_back.astype(jnp.bfloat16), "mp").astype(jnp.float32)
    slope_middle = (back_middle * silu_slope(pre_middle)).astype(jnp.bfloat16)
    raw_middle = jnp.dot(act_first.T, slope_middle, preferred_element_type=jnp.float32)
    back_first = jnp.dot(slope_middle, w_middle.T, preferred_element_type=jnp.float32)
    slope_first = (back_first * silu_slope(pre_first)).astype(jnp.bfloat16)
    raw_first = jnp.dot(belief.T, slope_first, preferred_element_type=jnp.float32)
    return (raw_first, raw_middle, raw_last)


def per_device(belief, target_value, counts, w_first, w_middle, w_last):
    total_rows = belief.shape[0]
    own_width = w_last.shape[1]
    target_value = lax.dynamic_slice_in_dim(
        target_value, lax.axis_index("mp") * own_width, own_width, 1
    )
    live_rows = (counts[:, None] > jnp.arange(BLOCK, dtype=jnp.int32)[None, :]).reshape(total_rows)
    raw_first, raw_middle, raw_last = rows_grads(
        belief, target_value, live_rows.astype(jnp.float32), w_first, w_middle, w_last
    )
    shard_first, shard_middle = (
        sum_at_owner(raw_first.astype(jnp.bfloat16), DP, 1),
        sum_at_owner(raw_middle.astype(jnp.bfloat16), DP, 1),
    )
    shard_last = sum_at_owner(raw_last.astype(jnp.bfloat16), DP, 0)
    local_squares = (
        jnp.sum(shard_first * shard_first)
        + jnp.sum(shard_middle * shard_middle)
        + jnp.sum(shard_last * shard_last)
    )
    square_sum = one_axis_at_a_time(local_squares, DP_MP)
    norm_scale = lax.rsqrt(square_sum / PARAMS + 1e-06)
    return (shard_first * norm_scale, shard_middle * norm_scale, shard_last * norm_scale)


def solution(mesh):
    finer = Mesh(
        mesh.devices.reshape(4, 2, 4, 2, mesh.shape["mp"]), ("dp_0", "dp_1", "dp_2", "dp_3", "mp")
    )
    return jax.shard_map(
        per_device,
        mesh=finer,
        in_specs=(P(DP, None), P(DP, None), P(DP), P(None, "mp"), P("mp", None), P(None, "mp")),
        out_specs=(P(None, MP_DP), P("mp", DP), P(DP, "mp")),
        check_vma=False,
    )
```

profile of v0, /device:TPU:0, one launch (start us, length us, event | category | flops | bytes accessed | tf_op | source)
XLA Modules:
  0.0 262.5 jit_solution(7464437599135056884)
XLA Ops:
  0.6 0.0 copy-start
  0.6 4.0 %fusion.12 = f32[256,768]{1,0:T(8,128)S(1)} fusion(bf16[256,2652]{0,1:T(8,128)(2,1)} %param.6, bf16[2652,768]{1,0:T(8,128)(2,1)} %param.9), kind=kOutput, calls=%fused_computation.36 | convolution fusion | flops 1042808832 | bytes 6217728 | tf_op jit(solution)/shard_map/dot_general | solution.py:49
  4.7 0.0 copy-start.6
  4.7 0.9 copy-done.6
  5.6 0.0 copy-done
  5.6 0.8 convolution_convert_fusion.3
  6.4 1.2 broadcast_in_dim.4
  7.7 0.0 copy-start.5
  7.7 4.7 %all-to-all-start = ((bf16[2,256,1536]{2,1,0:T(8,128)(2,1)}), bf16[2,256,1536]{2,1,0:T(8,128)(2,1)}, u32[]{:S(2)}, u32[]{:S(2)}) async-start(bf16[2,256,1536]{2,1,0:T(8,128)(2,1)} %broadcast_in_dim.4), calls=%async_computation | async-start | bytes 3145728 | tf_op jit(solution)/shard_map/all_to_all | solution.py:16
  12.4 0.0 copy-done.5
  12.4 0.1 fusion.10
  12.5 0.0 copy-start.4
  12.5 19.8 %all-to-all-done = bf16[2,256,1536]{2,1,0:T(8,128)(2,1)} async-done(((bf16[2,256,1536]{2,1,0:T(8,128)(2,1)}), bf16[2,256,1536]{2,1,0:T(8,128)(2,1)}, u32[]{:S(2)}, u32[]{:S(2)}) %all-to-all-start) | async-done | bytes 1572896 | tf_op jit(solution)/shard_map/all_to_all | solution.py:16
  32.3 0.0 copy-start.3
  32.3 2.0 convert_reduce_fusion.4
  34.2 0.0 copy-done.4
  34.3 0.0 copy-done.3
  34.3 0.0 copy-start.1
  34.3 0.9 fusion.4
  35.2 0.3 copy-done.1
  35.4 0.8 convolution_convert_fusion.4
  36.3 1.3 broadcast_in_dim.5
  37.6 4.6 %all-to-all-start.1 = ((bf16[2,256,1536]{2,1,0:T(8,128)(2,1)}), bf16[2,256,1536]{2,1,0:T(8,128)(2,1)}, u32[]{:S(2)}, u32[]{:S(2)}) async-start(bf16[2,256,1536]{2,1,0:T(8,128)(2,1)} %broadcast_in_dim.5), calls=%async_computation.1 | async-start | bytes 3145728 | tf_op jit(solution)/shard_map/all_to_all | solution.py:16
  42.2 3.5 %convolution_convert_fusion.2 = bf16[1536,663]{0,1:T(8,128)(2,1)} fusion(bf16[256,663]{0,1:T(8,128)(2,1)S(1)} %fusion.4, f32[256,1536]{1,0:T(8,128)} %copy-done.1), kind=kOutput, calls=%fused_computation.6 | convolution fusion | flops 524388864 | bytes 3949056 | tf_op jit(solution)/shard_map/dot_general | solution.py:57
  45.7 4.1 %copy.14 = bf16[1536,663]{1,0:T(8,128)(2,1)} copy(bf16[1536,663]{0,1:T(8,128)(2,1)} %convolution_convert_fusion.2) | data formatting | bytes 4073472 | tf_op jit(solution)/shard_map/convert_element_type | solution.py:82
  49.9 11.3 %all-to-all-done.1 = bf16[2,256,1536]{2,1,0:T(8,128)(2,1)} async-done(((bf16[2,256,1536]{2,1,0:T(8,128)(2,1)}), bf16[2,256,1536]{2,1,0:T(8,128)(2,1)}, u32[]{:S(2)}, u32[]{:S(2)}) %all-to-all-start.1) | async-done | bytes 1572896 | tf_op jit(solution)/shard_map/all_to_all | solution.py:16
  61.2 11.0 %all-to-all-start.4 = ((bf16[64,24,663]{2,1,0:T(8,128)(2,1)}), bf16[64,24,663]{2,1,0:T(8,128)(2,1)}, u32[]{:S(2)}, u32[]{:S(2)}) async-start(bf16[64,24,663]{2,1,0:T(8,128)(2,1)} %bitcast.23), calls=%async_computation.4 | async-start | bytes 4718592 | tf_op jit(solution)/shard_map/all_to_all | solution.py:33
  72.2 0.0 copy-start.2
  72.2 2.0 convert_reduce_fusion.3
  74.2 0.0 copy-done.2
  74.2 0.0 copy-start.7
  74.2 0.6 multiply_convert_fusion
  74.8 0.5 copy-done.7
  75.3 2.3 convolution_convert_fusion.1
  77.6 4.3 %copy.13 = bf16[768,1536]{0,1:T(8,128)(2,1)} copy(bf16[768,1536]{1,0:T(8,128)(2,1)} %convolution_convert_fusion.1) | data formatting | bytes 4718592 | tf_op jit(solution)/shard_map/convert_element_type | solution.py:80
  81.9 23.4 %all-to-all-done.4 = bf16[64,24,663]{2,1,0:T(8,128)(2,1)} async-done(((bf16[64,24,663]{2,1,0:T(8,128)(2,1)}), bf16[64,24,663]{2,1,0:T(8,128)(2,1)}, u32[]{:S(2)}, u32[]{:S(2)}) %all-to-all-start.4) | async-done | bytes 2036768 | tf_op jit(solution)/shard_map/all_to_all | solution.py:33
  105.3 5.5 %all-to-all-start.3 = ((bf16[64,768,24]{1,2,0:T(8,128)(2,1)}), bf16[64,768,24]{1,2,0:T(8,128)(2,1)}, u32[]{:S(2)}, u32[]{:S(2)}) async-start(bf16[64,768,24]{1,2,0:T(8,128)(2,1)} %bitcast.24), calls=%async_computation.3 | async-start | bytes 4718592 | tf_op jit(solution)/shard_map/all_to_all | solution.py:33
  110.8 5.5 %fusion = bf16[2652,768]{1,0:T(8,128)(2,1)} fusion(bf16[256,2652]{0,1:T(8,128)(2,1)} %param.6, bf16[256,1536]{1,0:T(8,128)(2,1)S(1)} %multiply_convert_fusion, bf16[768,1536]{1,0:T(8,128)(2,1)S(1)} %copy-done, f32[256,768]{1,0:T(8,128)} %copy-done.6), kind=kOutput, calls=%fused_computation.4 | convolution fusion | flops 1650594816 | bytes 9363456 | tf_op jit(solution)/shard_map/dot_general | solution.py:64
  116.3 6.4 %copy.12 = bf16[2652,768]{0,1:T(8,128)(2,1)} copy(bf16[2652,768]{1,0:T(8,128)(2,1)} %fusion) | data formatting | bytes 8146944 | tf_op jit(solution)/shard_map/convert_element_type | solution.py:79
  122.7 7.1 %reshape.34 = bf16[2652,64,12]{0,2,1:T(8,128)(2,1)} reshape(bf16[2652,768]{0,1:T(8,128)(2,1)} %copy.12) | data formatting | bytes 8146944 | tf_op jit(solution)/shard_map/reshape | solution.py:27
  129.9 14.0 %all-to-all-done.3 = bf16[64,768,24]{1,2,0:T(8,128)(2,1)} async-done(((bf16[64,768,24]{1,2,0:T(8,128)(2,1)}), bf16[64,768,24]{1,2,0:T(8,128)(2,1)}, u32[]{:S(2)}, u32[]{:S(2)}) %all-to-all-start.3) | async-done | bytes 2359328 | tf_op jit(solution)/shard_map/all_to_all | solution.py:33
  143.9 5.9 %all-to-all-start.2 = ((bf16[64,2652,12]{1,2,0:T(8,128)(2,1)}), bf16[64,2652,12]{1,2,0:T(8,128)(2,1)}, u32[]{:S(2)}, u32[]{:S(2)}) async-start(bf16[64,2652,12]{1,2,0:T(8,128)(2,1)} %bitcast.22), calls=%async_computation.2 | async-start | bytes 11010048 | tf_op jit(solution)/shard_map/all_to_all | solution.py:33
  149.8 2.0 convert_reduce_fusion.1
  151.8 0.6 multiply_reduce_fusion.1
  152.4 2.0 convert_reduce_fusion.2
  154.5 0.6 multiply_reduce_fusion.2
  155.1 62.1 %all-to-all-done.2 = bf16[64,2652,12]{1,2,0:T(8,128)(2,1)} async-done(((bf16[64,2652,12]{1,2,0:T(8,128)(2,1)}), bf16[64,2652,12]{1,2,0:T(8,128)(2,1)}, u32[]{:S(2)}, u32[]{:S(2)}) %all-to-all-start.2) | async-done | bytes 4073504 | tf_op jit(solution)/shard_map/all_to_all | solution.py:33
  217.2 3.5 %convert_reduce_fusion = f32[2652,12]{0,1:T(8,128)S(1)} fusion(bf16[64,2652,12]{1,2,0:T(8,128)(2,1)} %all-to-all-done.2), kind=kLoop, calls=%fused_computation | loop fusion | flops 4041648 | bytes 4200768 | tf_op jit(solution)/shard_map/reduce_sum | solution.py:34
  220.7 0.6 multiply_reduce_fusion
  223.3 10.2 %psum.35 = f32[]{:T(128)} all-reduce(f32[]{:T(128)S(6)} %add.44), channel_id=1, replica_groups=mesh['dp_0'=4,'dp_1'=2,'dp_2'=4,'dp_3'=2,'mp'=2] {'dp_0'}, use_global_device_ids=true, to_apply=%region_8.9 | all-reduce | flops 1 | bytes 8 | tf_op jit(solution)/shard_map/psum | solution.py:39
  233.5 7.1 %psum.36 = f32[]{:T(128)} all-reduce(f32[]{:T(128)} %psum.35), channel_id=1, replica_groups=mesh['dp_0'=4,'dp_1'=2,'dp_2'=4,'dp_3'=2,'mp'=2] {'dp_1'}, use_global_device_ids=true, to_apply=%region_9.10 | all-reduce | flops 1 | bytes 8 | tf_op jit(solution)/shard_map/psum | solution.py:39
  240.6 10.6 %psum.37 = f32[]{:T(128)} all-reduce(f32[]{:T(128)} %psum.36), channel_id=1, replica_groups=mesh['dp_0'=4,'dp_1'=2,'dp_2'=4,'dp_3'=2,'mp'=2] {'dp_2'}, use_global_device_ids=true, to_apply=%region_10.11 | all-reduce | flops 1 | bytes 8 | tf_op jit(solution)/shard_map/psum | solution.py:39
  251.2 3.1 %psum.38 = f32[]{:T(128)} all-reduce(f32[]{:T(128)} %psum.37), channel_id=1, replica_groups=mesh['dp_0'=4,'dp_1'=2,'dp_2'=4,'dp_3'=2,'mp'=2] {'dp_3'}, use_global_device_ids=true, to_apply=%region_11.12 | all-reduce | flops 1 | bytes 8 | tf_op jit(solution)/shard_map/psum | solution.py:39
  254.3 5.5 %psum.39 = f32[]{:T(128)} all-reduce(f32[]{:T(128)} %psum.38), channel_id=1, replica_groups=mesh['dp_0'=4,'dp_1'=2,'dp_2'=4,'dp_3'=2,'mp'=2] {'mp'}, use_global_device_ids=true, to_apply=%region_12.13 | all-reduce | flops 1 | bytes 8 | tf_op jit(solution)/shard_map/psum | solution.py:39
  260.5 0.6 broadcast_multiply_fusion.1
  261.1 0.6 broadcast_multiply_fusion.2
  261.8 0.7 broadcast_multiply_fusion
Async XLA Ops:
  0.6 5.0 %copy-start = (bf16[768,1536]{1,0:T(8,128)(2,1)S(1)}, bf16[768,1536]{1,0:T(8,128)(2,1)}, u32[]{:S(2)}) copy-start(bf16[768,1536]{1,0:T(8,128)(2,1)} %param.10) | copy-start | bytes 7077892
  4.7 0.9 copy-start.6
  7.7 4.7 %copy-start.5 = (s32[2]{0:T(128)S(1)}, s32[2]{0:T(128)}, u32[]{:S(2)}) copy-start(s32[2]{0:T(128)} %param.8) | copy-start | bytes 28
  7.7 24.6 %all-to-all-start = ((bf16[2,256,1536]{2,1,0:T(8,128)(2,1)}), bf16[2,256,1536]{2,1,0:T(8,128)(2,1)}, u32[]{:S(2)}, u32[]{:S(2)}) async-start(bf16[2,256,1536]{2,1,0:T(8,128)(2,1)} %broadcast_in_dim.4), calls=%async_computation | async-start | bytes 3145728 | tf_op jit(solution)/shard_map/all_to_all | solution.py:16
  12.5 21.8 %copy-start.4 = (bf16[256,1326]{0,1:T(8,128)(2,1)S(1)}, bf16[256,1326]{0,1:T(8,128)(2,1)}, u32[]{:S(2)}) copy-start(bf16[256,1326]{0,1:T(8,128)(2,1)} %param.7) | copy-start | bytes 2036740
  32.3 2.0 copy-start.3
  34.3 1.1 copy-start.1
  37.6 23.6 %all-to-all-start.1 = ((bf16[2,256,1536]{2,1,0:T(8,128)(2,1)}), bf16[2,256,1536]{2,1,0:T(8,128)(2,1)}, u32[]{:S(2)}, u32[]{:S(2)}) async-start(bf16[2,256,1536]{2,1,0:T(8,128)(2,1)} %broadcast_in_dim.5), calls=%async_computation.1 | async-start | bytes 3145728 | tf_op jit(solution)/shard_map/all_to_all | solution.py:16
  61.2 44.1 %all-to-all-start.4 = ((bf16[64,24,663]{2,1,0:T(8,128)(2,1)}), bf16[64,24,663]{2,1,0:T(8,128)(2,1)}, u32[]{:S(2)}, u32[]{:S(2)}) async-start(bf16[64,24,663]{2,1,0:T(8,128)(2,1)} %bitcast.23), calls=%async_computation.4 | async-start | bytes 4718592 | tf_op jit(solution)/shard_map/all_to_all | solution.py:33
  72.2 2.0 copy-start.2
  74.2 1.1 copy-start.7
  105.3 38.6 %all-to-all-start.3 = ((bf16[64,768,24]{1,2,0:T(8,128)(2,1)}), bf16[64,768,24]{1,2,0:T(8,128)(2,1)}, u32[]{:S(2)}, u32[]{:S(2)}) async-start(bf16[64,768,24]{1,2,0:T(8,128)(2,1)} %bitcast.24), calls=%async_computation.3 | async-start | bytes 4718592 | tf_op jit(solution)/shard_map/all_to_all | solution.py:33
  143.9 73.3 %all-to-all-start.2 = ((bf16[64,2652,12]{1,2,0:T(8,128)(2,1)}), bf16[64,2652,12]{1,2,0:T(8,128)(2,1)}, u32[]{:S(2)}, u32[]{:S(2)}) async-start(bf16[64,2652,12]{1,2,0:T(8,128)(2,1)} %bitcast.22), calls=%async_computation.2 | async-start | bytes 11010048 | tf_op jit(solution)/shard_map/all_to_all | solution.py:33
where the time goes:
time: 264 us; the launch traced here: 262 us
  waiting for transfers between devices  131 us (50%)
  blocking collectives  36.5 us (14%)
  starting transfers between devices  31.7 us (12%)
  local copies, waits for them, and re-layouts  26.3 us (10%)
  matrix products  17.8 us (7%)
  other arithmetic  16 us (6%)
  between operations  3.43 us (1%)
    all_to_all x3, waiting for transfers between devices, sum_at_owner(): blocks = lax.all_to_all(cut_along(shard, dim, size), axis, 0, 0, tiled=True)  99.5 us
    psum x5, blocking collectives, one_axis_at_a_time(): shard = lax.psum(shard, axis)  36.5 us
    all_to_all x2, waiting for transfers between devices, copy_for_each(): lax.all_to_all(jnp.broadcast_to(shard[None], (size, *shard.shape)), axis,...  31.1 us
    all_to_all x3, starting transfers between devices, sum_at_owner(): blocks = lax.all_to_all(cut_along(shard, dim, size), axis, 0, 0, tiled=True)  22.4 us
    all_to_all x2, starting transfers between devices, copy_for_each(): lax.all_to_all(jnp.broadcast_to(shard[None], (size, *shard.shape)), axis,...  9.34 us
    reduce_sum x3, other arithmetic, sum_at_owner(): return jnp.sum(blocks.astype(jnp.float32), axis=0)  7.58 us
    reshape x1, local copies, waits for them, and re-layouts, cut_along(): shard.reshape(*lengths[:dim], size, lengths[dim] // size, *lengths[dim +...  7.11 us
    convert_element_type x1, local copies, waits for them, and re-layouts, per_device(): raw_first.astype(jnp.bfloat16)  6.42 us
  transfers between devices with their start and end apart: 5, of which 5 were waited for; matrix products, arithmetic and copies ran while one was open for 16% of the time, Pallas kernels for 0%

commit v1 on v0

--- a/solution.py
+++ b/solution.py
@@ -36,7 +36,8 @@
 
 def one_axis_at_a_time(shard, axes):
     for axis in axes:
-        shard = lax.psum(shard, axis)
+        pieces = lax.all_gather(shard, axis, axis=0, tiled=False)
+        shard = pieces.sum(axis=0)
     return shard
 
 

time: 264 us -> 273 us (1.034)
  local copies, waits for them, and re-layouts: 26.3 us -> 35.6 us
  blocking collectives: 36.5 us -> 33.4 us
  other arithmetic: 16 us -> 19 us
    psum x5 -> x0, blocking collectives: 36.5 us -> none  [one_axis_at_a_time(): shard = lax.psum(shard, axis)]
    unnamed x0 -> x5, blocking collectives: none -> 33.4 us
    unnamed x16 -> x41, local copies, waits for them, and re-layouts: 1.77 us -> 11.1 us
    reduce_sum x0 -> x5, other arithmetic: none -> 3.02 us  [one_axis_at_a_time(): shard = pieces.sum(axis=0)]
  transfers between devices with their start and end apart: 5 -> 5, of which waited for: 5 -> 5; matrix products, arithmetic and copies ran while one was open for 16% -> 15% of each run, Pallas kernels for 0% -> 0%
where the time goes in v1:
time: 273 us; the launch traced here: 271 us
  waiting for transfers between devices  130 us (48%)
  local copies, waits for them, and re-layouts  35.6 us (13%)
  blocking collectives  33.4 us (12%)
  starting transfers between devices  31.9 us (12%)
  other arithmetic  19 us (7%)
  matrix products  17.8 us (7%)
  between operations  3.47 us (1%)
    all_to_all x3, waiting for transfers between devices, sum_at_owner(): blocks = lax.all_to_all(cut_along(shard, dim, size), axis, 0, 0, tiled=True)  98.9 us
    unnamed x5, blocking collectives  33.4 us
    all_to_all x2, waiting for transfers between devices, copy_for_each(): lax.all_to_all(jnp.broadcast_to(shard[None], (size, *shard.shape)), axis,...  31.1 us
    all_to_all x3, starting transfers between devices, sum_at_owner(): blocks = lax.all_to_all(cut_along(shard, dim, size), axis, 0, 0, tiled=True)  22.5 us
    unnamed x41, local copies, waits for them, and re-layouts  11.1 us
    all_to_all x2, starting transfers between devices, copy_for_each(): lax.all_to_all(jnp.broadcast_to(shard[None], (size, *shard.shape)), axis,...  9.34 us
    reduce_sum x3, other arithmetic, sum_at_owner(): return jnp.sum(blocks.astype(jnp.float32), axis=0)  7.58 us
    reshape x1, local copies, waits for them, and re-layouts, cut_along(): shard.reshape(*lengths[:dim], size, lengths[dim] // size, *lengths[dim +...  7.11 us
  transfers between devices with their start and end apart: 5, of which 5 were waited for; matrix products, arithmetic and copies ran while one was open for 15% of the time, Pallas kernels for 0%

profile of v1, /device:TPU:0, one launch (start us, length us, event | category | flops | bytes accessed | tf_op | source)
XLA Modules:
  0.0 271.3 jit_solution(6612197896418310964)
XLA Ops:
  0.6 0.0 copy-start
  0.6 4.0 %fusion.12 = f32[256,768]{1,0:T(8,128)S(1)} fusion(bf16[256,2652]{0,1:T(8,128)(2,1)} %param.6, bf16[2652,768]{1,0:T(8,128)(2,1)} %param.9), kind=kOutput, calls=%fused_computation.36 | convolution fusion | flops 1042808832 | bytes 6217728 | tf_op jit(solution)/shard_map/dot_general | solution.py:50
  4.7 0.9 copy-done.11
  5.6 0.8 convolution_convert_fusion.3
  6.4 1.2 broadcast_in_dim.4
  7.7 4.7 %all-to-all-start = ((bf16[2,256,1536]{2,1,0:T(8,128)(2,1)}), bf16[2,256,1536]{2,1,0:T(8,128)(2,1)}, u32[]{:S(2)}, u32[]{:S(2)}) async-start(bf16[2,256,1536]{2,1,0:T(8,128)(2,1)} %broadcast_in_dim.4), calls=%async_computation | async-start | bytes 3145728 | tf_op jit(solution)/shard_map/all_to_all | solution.py:16
  12.4 0.1 fusion.10
  12.5 19.8 %all-to-all-done = bf16[2,256,1536]{2,1,0:T(8,128)(2,1)} async-done(((bf16[2,256,1536]{2,1,0:T(8,128)(2,1)}), bf16[2,256,1536]{2,1,0:T(8,128)(2,1)}, u32[]{:S(2)}, u32[]{:S(2)}) %all-to-all-start) | async-done | bytes 1572896 | tf_op jit(solution)/shard_map/all_to_all | solution.py:16
  32.3 2.0 convert_reduce_fusion.4
  34.3 0.0 copy-done.3
  34.3 0.9 fusion.4
  35.2 0.3 copy-done.1
  35.4 0.8 convolution_convert_fusion.4
  36.3 1.3 broadcast_in_dim.5
  37.6 4.6 %all-to-all-start.1 = ((bf16[2,256,1536]{2,1,0:T(8,128)(2,1)}), bf16[2,256,1536]{2,1,0:T(8,128)(2,1)}, u32[]{:S(2)}, u32[]{:S(2)}) async-start(bf16[2,256,1536]{2,1,0:T(8,128)(2,1)} %broadcast_in_dim.5), calls=%async_computation.1 | async-start | bytes 3145728 | tf_op jit(solution)/shard_map/all_to_all | solution.py:16
  42.2 3.5 %convolution_convert_fusion.2 = bf16[1536,663]{0,1:T(8,128)(2,1)} fusion(bf16[256,663]{0,1:T(8,128)(2,1)S(1)} %fusion.4, f32[256,1536]{1,0:T(8,128)} %copy-done.1), kind=kOutput, calls=%fused_computation.6 | convolution fusion | flops 524388864 | bytes 3949056 | tf_op jit(solution)/shard_map/dot_general | solution.py:58
  45.7 4.1 %copy.14 = bf16[1536,663]{1,0:T(8,128)(2,1)} copy(bf16[1536,663]{0,1:T(8,128)(2,1)} %convolution_convert_fusion.2) | data formatting | bytes 4073472 | tf_op jit(solution)/shard_map/convert_element_type | solution.py:83
  49.9 11.3 %all-to-all-done.1 = bf16[2,256,1536]{2,1,0:T(8,128)(2,1)} async-done(((bf16[2,256,1536]{2,1,0:T(8,128)(2,1)}), bf16[2,256,1536]{2,1,0:T(8,128)(2,1)}, u32[]{:S(2)}, u32[]{:S(2)}) %all-to-all-start.1) | async-done | bytes 1572896 | tf_op jit(solution)/shard_map/all_to_all | solution.py:16
  61.2 11.0 %all-to-all-start.4 = ((bf16[64,24,663]{2,1,0:T(8,128)(2,1)}), bf16[64,24,663]{2,1,0:T(8,128)(2,1)}, u32[]{:S(2)}, u32[]{:S(2)}) async-start(bf16[64,24,663]{2,1,0:T(8,128)(2,1)} %bitcast.33), calls=%async_computation.4 | async-start | bytes 4718592 | tf_op jit(solution)/shard_map/all_to_all | solution.py:33
  72.2 2.0 convert_reduce_fusion.3
  74.2 0.6 multiply_convert_fusion
  74.8 0.5 copy-done.12
  75.3 2.3 convolution_convert_fusion.1
  77.6 4.3 %copy.13 = bf16[768,1536]{0,1:T(8,128)(2,1)} copy(bf16[768,1536]{1,0:T(8,128)(2,1)} %convolution_convert_fusion.1) | data formatting | bytes 4718592 | tf_op jit(solution)/shard_map/convert_element_type | solution.py:81
  81.9 23.4 %all-to-all-done.4 = bf16[64,24,663]{2,1,0:T(8,128)(2,1)} async-done(((bf16[64,24,663]{2,1,0:T(8,128)(2,1)}), bf16[64,24,663]{2,1,0:T(8,128)(2,1)}, u32[]{:S(2)}, u32[]{:S(2)}) %all-to-all-start.4) | async-done | bytes 2036768 | tf_op jit(solution)/shard_map/all_to_all | solution.py:33
  105.3 5.5 %all-to-all-start.3 = ((bf16[64,768,24]{1,2,0:T(8,128)(2,1)}), bf16[64,768,24]{1,2,0:T(8,128)(2,1)}, u32[]{:S(2)}, u32[]{:S(2)}) async-start(bf16[64,768,24]{1,2,0:T(8,128)(2,1)} %bitcast.34), calls=%async_computation.3 | async-start | bytes 4718592 | tf_op jit(solution)/shard_map/all_to_all | solution.py:33
  110.8 5.5 %fusion = bf16[2652,768]{1,0:T(8,128)(2,1)} fusion(bf16[256,2652]{0,1:T(8,128)(2,1)} %param.6, bf16[256,1536]{1,0:T(8,128)(2,1)S(1)} %multiply_convert_fusion, bf16[768,1536]{1,0:T(8,128)(2,1)S(1)} %copy-done, f32[256,768]{1,0:T(8,128)} %copy-done.11), kind=kOutput, calls=%fused_computation.4 | convolution fusion | flops 1650594816 | bytes 9363456 | tf_op jit(solution)/shard_map/dot_general | solution.py:65
  116.3 6.4 %copy.12 = bf16[2652,768]{0,1:T(8,128)(2,1)} copy(bf16[2652,768]{1,0:T(8,128)(2,1)} %fusion) | data formatting | bytes 8146944 | tf_op jit(solution)/shard_map/convert_element_type | solution.py:80
  122.7 7.1 %reshape.34 = bf16[2652,64,12]{0,2,1:T(8,128)(2,1)} reshape(bf16[2652,768]{0,1:T(8,128)(2,1)} %copy.12) | data formatting | bytes 8146944 | tf_op jit(solution)/shard_map/reshape | solution.py:27
  129.9 14.0 %all-to-all-done.3 = bf16[64,768,24]{1,2,0:T(8,128)(2,1)} async-done(((bf16[64,768,24]{1,2,0:T(8,128)(2,1)}), bf16[64,768,24]{1,2,0:T(8,128)(2,1)}, u32[]{:S(2)}, u32[]{:S(2)}) %all-to-all-start.3) | async-done | bytes 2359328 | tf_op jit(solution)/shard_map/all_to_all | solution.py:33
  143.9 6.0 %all-to-all-start.2 = ((bf16[64,2652,12]{1,2,0:T(8,128)(2,1)}), bf16[64,2652,12]{1,2,0:T(8,128)(2,1)}, u32[]{:S(2)}, u32[]{:S(2)}) async-start(bf16[64,2652,12]{1,2,0:T(8,128)(2,1)} %bitcast.32), calls=%async_computation.2 | async-start | bytes 11010048 | tf_op jit(solution)/shard_map/all_to_all | solution.py:33
  149.9 0.0 copy-done.10
  149.9 0.6 dynamic-slice
  150.5 2.0 convert_reduce_fusion.1
  152.6 0.6 multiply_reduce_fusion.1
  153.2 2.0 convert_reduce_fusion.2
  155.2 0.6 multiply_reduce_fusion.2
  155.8 61.5 %all-to-all-done.2 = bf16[64,2652,12]{1,2,0:T(8,128)(2,1)} async-done(((bf16[64,2652,12]{1,2,0:T(8,128)(2,1)}), bf16[64,2652,12]{1,2,0:T(8,128)(2,1)}, u32[]{:S(2)}, u32[]{:S(2)}) %all-to-all-start.2) | async-done | bytes 4073504 | tf_op jit(solution)/shard_map/all_to_all | solution.py:33
  217.3 3.5 %convert_reduce_fusion = f32[2652,12]{0,1:T(8,128)S(1)} fusion(bf16[64,2652,12]{1,2,0:T(8,128)(2,1)} %all-to-all-done.2), kind=kLoop, calls=%fused_computation | loop fusion | flops 4041648 | bytes 4200768 | tf_op jit(solution)/shard_map/reduce_sum | solution.py:34
  220.8 0.6 multiply_reduce_fusion
  223.4 0.7 dynamic-update-slice
  224.2 0.0 copy-done.9
  224.2 0.6 dynamic-slice.1
  224.8 9.7 %all-reduce = f32[4]{0:T(128)S(1)} all-reduce(f32[4]{0:T(128)S(1)} %dynamic-update-slice), channel_id=1, replica_groups=mesh['dp_0'=4,'dp_1'=2,'dp_2'=4,'dp_3'=2,'mp'=2] {'dp_0'}, use_global_device_ids=true, to_apply=%add | all-reduce | flops 4 | bytes 32
  234.4 0.6 reduce_sum.125
  235.0 1.4 dynamic-update-slice.1
  236.4 0.6 dynamic-slice.2
  237.0 6.4 %all-reduce.1 = f32[2]{0:T(128)S(1)} all-reduce(f32[2]{0:T(128)S(1)} %dynamic-update-slice.1), channel_id=1, replica_groups=mesh['dp_0'=4,'dp_1'=2,'dp_2'=4,'dp_3'=2,'mp'=2] {'dp_1'}, use_global_device_ids=true, to_apply=%add.1 | all-reduce | flops 2 | bytes 16
  243.5 0.6 reduce_sum.126
  244.1 1.4 dynamic-update-slice.2
  245.5 0.6 dynamic-slice.3
  246.0 10.0 %all-reduce.2 = f32[4]{0:T(128)S(1)} all-reduce(f32[4]{0:T(128)S(1)} %dynamic-update-slice.2), channel_id=1, replica_groups=mesh['dp_0'=4,'dp_1'=2,'dp_2'=4,'dp_3'=2,'mp'=2] {'dp_2'}, use_global_device_ids=true, to_apply=%add.2 | all-reduce | flops 4 | bytes 32
  256.0 0.6 reduce_sum.127
  256.6 1.4 dynamic-update-slice.3
  258.0 0.0 copy-done.6
  258.0 0.6 dynamic-slice.4
  258.6 2.4 all-reduce.3
  261.1 0.6 reduce_sum.128
  261.7 1.4 dynamic-update-slice.4
  263.1 4.9 %all-reduce.4 = f32[2]{0:T(128)S(1)} all-reduce(f32[2]{0:T(128)S(1)} %dynamic-update-slice.4), channel_id=1, replica_groups=mesh['dp_0'=4,'dp_1'=2,'dp_2'=4,'dp_3'=2,'mp'=2] {'mp'}, use_global_device_ids=true, to_apply=%add.4 | all-reduce | flops 2 | bytes 16
  268.0 0.6 reduce_sum.129
  269.3 0.6 broadcast_multiply_fusion.1
  269.9 0.6 broadcast_multiply_fusion.2
  270.6 0.7 broadcast_multiply_fusion
  (23 shorter events, 0.0 us)
Async XLA Ops:
  0.6 5.0 %copy-start = (bf16[768,1536]{1,0:T(8,128)(2,1)S(1)}, bf16[768,1536]{1,0:T(8,128)(2,1)}, u32[]{:S(2)}) copy-start(bf16[768,1536]{1,0:T(8,128)(2,1)} %param.10) | copy-start | bytes 7077892
  4.7 0.9 copy-start.11
  7.7 4.7 %copy-start.5 = (s32[2]{0:T(128)S(1)}, s32[2]{0:T(128)}, u32[]{:S(2)}) copy-start(s32[2]{0:T(128)} %param.8) | copy-start | bytes 28
  7.7 24.6 %all-to-all-start = ((bf16[2,256,1536]{2,1,0:T(8,128)(2,1)}), bf16[2,256,1536]{2,1,0:T(8,128)(2,1)}, u32[]{:S(2)}, u32[]{:S(2)}) async-start(bf16[2,256,1536]{2,1,0:T(8,128)(2,1)} %broadcast_in_dim.4), calls=%async_computation | async-start | bytes 3145728 | tf_op jit(solution)/shard_map/all_to_all | solution.py:16
  12.5 21.8 %copy-start.4 = (bf16[256,1326]{0,1:T(8,128)(2,1)S(1)}, bf16[256,1326]{0,1:T(8,128)(2,1)}, u32[]{:S(2)}) copy-start(bf16[256,1326]{0,1:T(8,128)(2,1)} %param.7) | copy-start | bytes 2036740
  32.3 2.0 copy-start.3
  34.3 1.1 copy-start.1
  37.6 23.6 %all-to-all-start.1 = ((bf16[2,256,1536]{2,1,0:T(8,128)(2,1)}), bf16[2,256,1536]{2,1,0:T(8,128)(2,1)}, u32[]{:S(2)}, u32[]{:S(2)}) async-start(bf16[2,256,1536]{2,1,0:T(8,128)(2,1)} %broadcast_in_dim.5), calls=%async_computation.1 | async-start | bytes 3145728 | tf_op jit(solution)/shard_map/all_to_all | solution.py:16
  61.2 44.1 %all-to-all-start.4 = ((bf16[64,24,663]{2,1,0:T(8,128)(2,1)}), bf16[64,24,663]{2,1,0:T(8,128)(2,1)}, u32[]{:S(2)}, u32[]{:S(2)}) async-start(bf16[64,24,663]{2,1,0:T(8,128)(2,1)} %bitcast.33), calls=%async_computation.4 | async-start | bytes 4718592 | tf_op jit(solution)/shard_map/all_to_all | solution.py:33
  72.2 2.0 copy-start.2
  74.2 1.1 copy-start.12
  105.3 38.6 %all-to-all-start.3 = ((bf16[64,768,24]{1,2,0:T(8,128)(2,1)}), bf16[64,768,24]{1,2,0:T(8,128)(2,1)}, u32[]{:S(2)}, u32[]{:S(2)}) async-start(bf16[64,768,24]{1,2,0:T(8,128)(2,1)} %bitcast.34), calls=%async_computation.3 | async-start | bytes 4718592 | tf_op jit(solution)/shard_map/all_to_all | solution.py:33
  143.9 6.0 %copy-start.10 = (u32[128]{0:T(128)S(1)}, u32[128]{0:T(128)}, u32[]{:S(2)}) copy-start(u32[128]{0:T(128)} %constant.31) | copy-start | bytes 1540
  143.9 73.4 %all-to-all-start.2 = ((bf16[64,2652,12]{1,2,0:T(8,128)(2,1)}), bf16[64,2652,12]{1,2,0:T(8,128)(2,1)}, u32[]{:S(2)}, u32[]{:S(2)}) async-start(bf16[64,2652,12]{1,2,0:T(8,128)(2,1)} %bitcast.32), calls=%async_computation.2 | async-start | bytes 11010048 | tf_op jit(solution)/shard_map/all_to_all | solution.py:33
  155.8 68.3 %copy-start.9 = (u32[128]{0:T(128)S(1)}, u32[128]{0:T(128)}, u32[]{:S(2)}) copy-start(u32[128]{0:T(128)} %constant.36) | copy-start | bytes 1540
  155.8 80.6 %copy-start.8 = (u32[128]{0:T(128)S(1)}, u32[128]{0:T(128)}, u32[]{:S(2)}) copy-start(u32[128]{0:T(128)} %constant.41) | copy-start | bytes 1540
  155.8 89.6 %copy-start.7 = (u32[128]{0:T(128)S(1)}, u32[128]{0:T(128)}, u32[]{:S(2)}) copy-start(u32[128]{0:T(128)} %constant.46) | copy-start | bytes 1540
  155.8 102.2 %copy-start.6 = (u32[128]{0:T(128)S(1)}, u32[128]{0:T(128)}, u32[]{:S(2)}) copy-start(u32[128]{0:T(128)} %constant.51) | copy-start | bytes 1540
